TPU v7x, 256 devices: a whole 4x4x8 slice. The times are simulated.
256 devices in a mesh: seq: 16 (over x, y), head: 16 (over z, core).
Axes of the slice: x: 4, y: 4, z: 8, core: 2. Of those that a mesh axis runs over, the one named last changes fastest.
Arguments:
- layer_input: bfloat16 [8192, 4096], P('seq', 'head'), may hold values from -40 to 40
- qk_weight: bfloat16 [4096, 4096], P('seq', 'head'), may hold values from -0.09375 to 0.09375
- value_weight: bfloat16 [4096, 4096], P('seq', 'head'), may hold values from -0.09375 to 0.09375
- groups: int32 [2, 8192, 1], P(None, 'seq'), may hold values from 0 to 15; in each aligned block of 512 rows (0 to 511, 512 to 1023, ..., all dimensions but the last counted through in order) at most 48 rows name the same one
- buckets: int32 [2, 8192], P(None, 'seq'), may hold values from 0 to 7
- out_cotangent: bfloat16 [8192, 4096], P('seq', 'head'), may hold values from -6 to 6
Outputs:
- output: bfloat16 [8192, 4096], P('seq', 'head')
- input_grad: bfloat16 [8192, 4096], P('seq', 'head')
- qk_weight_grad: float32 [4096, 4096], P('seq', 'head')
- value_weight_grad: float32 [4096, 4096], P('seq', 'head')
Inputs may be any that keep to these rules, and one draw needn't show every extreme that they name: `groups`: among the 512 tokens of one device in one round no group is named more than 48 times, and in every draw some device's tokens name some group exactly 48 times.
All inputs are finite; a program needn't handle non-finite values.
Results may differ from a plain program's by a relative error of at most 0.018.
The roundings to bfloat16 on the way count: a program that leaves them out, or rounds other values in their place, can miss the bound.
Values may be sent and summed in bfloat16 or wider, within the bound.
A program may use at most 128 MiB of HBM per device.

v0:
```python
import math
import jax
import jax.numpy as jnp
from jax import lax
from jax.sharding import PartitionSpec as P

HEAD_DIM = 128
ROUNDS = 2
BLOCK_LEN = 128
SUB_BUCKETS = 8
EPSILON = 1e-06
SELF_SCORE = -100000.0
MASKED_SCORE = -1000000000.0


def key_factor(query_f):
    return lax.rsqrt(jnp.mean(query_f * query_f, axis=-1, keepdims=True) + EPSILON) / math.sqrt(
        query_f.shape[-1]
    )


def with_previous(blocked):
    return jnp.concatenate([blocked, jnp.roll(blocked, 1, axis=0)], axis=1)


def fold_previous(block_grads, block_width):
    return block_grads[:, :block_width] + jnp.roll(block_grads[:, block_width:], -1, axis=0)


def attention_rows(queries, values, live_slots):
    slot_total, heads_here, head_width = queries.shape
    blocks = slot_total // BLOCK_LEN
    query_f = queries.astype(jnp.float32)
    factor = key_factor(query_f)
    normed = (query_f * factor).astype(jnp.bfloat16)
    query_blocks = queries.reshape(blocks, BLOCK_LEN, heads_here, head_width)
    key_blocks = with_previous(normed.reshape(blocks, BLOCK_LEN, heads_here, head_width))
    value_blocks = with_previous(values.reshape(blocks, BLOCK_LEN, heads_here, head_width))
    live_keys = with_previous(live_slots.reshape(blocks, BLOCK_LEN))
    self_pairs = jnp.arange(BLOCK_LEN)[:, None] == jnp.arange(2 * BLOCK_LEN)[None, :]
    scores = jnp.einsum(
        "nqhd,nkhd->nhqk", query_blocks, key_blocks, preferred_element_type=jnp.float32
    )
    scores = jnp.where(self_pairs, SELF_SCORE, scores)
    scores = jnp.where(live_keys[:, None, None, :], scores, MASKED_SCORE)
    largest = jnp.max(scores, axis=-1, keepdims=True)
    exponent = jnp.exp(scores - largest)
    row_total = jnp.sum(exponent, axis=-1, keepdims=True)
    weights = exponent / row_total
    log_total = (largest + jnp.log(row_total))[..., 0]
    return (weights, log_total, query_blocks, key_blocks, value_blocks, self_pairs, factor)


def forward_rows(queries, values, live_slots):
    slot_total, heads_here, head_width = queries.shape
    weights, log_total, query_blocks, key_blocks, value_blocks, self_pairs, factor = attention_rows(
        queries, values, live_slots
    )
    mixed_rows = jnp.einsum(
        "nhqk,nkhd->nqhd",
        weights.astype(jnp.bfloat16),
        value_blocks,
        preferred_element_type=jnp.float32,
    )
    return (
        mixed_rows.reshape(slot_total, heads_here, head_width),
        jnp.transpose(log_total, (0, 2, 1)).reshape(slot_total, heads_here),
    )


def backward_rows(queries, values, live_slots, out_grads, mixes, inners):
    slot_total, heads_here, head_width = queries.shape
    blocks = slot_total // BLOCK_LEN
    weights, log_total, query_blocks, key_blocks, value_blocks, self_pairs, factor = attention_rows(
        queries, values, live_slots
    )
    mix_blocks = jnp.transpose(mixes.reshape(blocks, BLOCK_LEN, heads_here), (0, 2, 1))[..., None]
    inner_blocks = jnp.transpose(inners.reshape(blocks, BLOCK_LEN, heads_here), (0, 2, 1))[
        ..., None
    ]
    scaled = (weights * mix_blocks).astype(jnp.bfloat16)
    grad_blocks = out_grads.reshape(blocks, BLOCK_LEN, heads_here, head_width)
    value_grads = fold_previous(
        jnp.einsum("nhqk,nqhd->nkhd", scaled, grad_blocks, preferred_element_type=jnp.float32),
        BLOCK_LEN,
    )
    pair_grads = jnp.einsum(
        "nqhd,nkhd->nhqk", grad_blocks, value_blocks, preferred_element_type=jnp.float32
    )
    score_grads = jnp.where(
        self_pairs, 0.0, weights * mix_blocks * (pair_grads - inner_blocks)
    ).astype(jnp.bfloat16)
    query_part = jnp.einsum(
        "nhqk,nkhd->nqhd", score_grads, key_blocks, preferred_element_type=jnp.float32
    ).reshape(slot_total, heads_here, head_width)
    key_part = fold_previous(
        jnp.einsum(
            "nhqk,nqhd->nkhd", score_grads, query_blocks, preferred_element_type=jnp.float32
        ),
        BLOCK_LEN,
    ).reshape(slot_total, heads_here, head_width)
    query_f = queries.astype(jnp.float32)
    result = (
        query_part
        + factor * key_part
        - factor * factor * factor * jnp.sum(key_part * query_f, axis=-1, keepdims=True) * query_f
    )
    return (
        result.astype(jnp.bfloat16),
        value_grads.reshape(slot_total, heads_here, head_width).astype(jnp.bfloat16),
    )


def spread_rows(token_rows, source_rows):
    padded = jnp.concatenate(
        [token_rows, jnp.zeros((1,) + token_rows.shape[1:], token_rows.dtype)], axis=0
    )
    return padded[source_rows]


def per_device(layer_input, qk_weight, value_weight, groups, buckets, out_cotangent):
    tokens_here = layer_input.shape[0]
    width_here = layer_input.shape[1]
    heads_here = width_here // HEAD_DIM
    seq_count = lax.axis_size("seq")
    token_total = tokens_here * seq_count
    capacity = 3 * tokens_here // (2 * seq_count)
    slot_count = seq_count * capacity
    features = lax.all_gather(layer_input, "head", axis=1, tiled=True)
    stacked = jnp.stack((qk_weight, value_weight))
    full_weights = lax.all_gather(stacked, "seq", axis=1, tiled=True)
    projected = jnp.einsum(
        "td,kdc->tkc", features, full_weights, preferred_element_type=jnp.float32
    )
    queries = projected[:, 0].astype(jnp.bfloat16).reshape(tokens_here, heads_here, HEAD_DIM)
    values = projected[:, 1].astype(jnp.bfloat16).reshape(tokens_here, heads_here, HEAD_DIM)
    position = lax.axis_index("seq") * tokens_here + jnp.arange(tokens_here, dtype=jnp.int32)
    sentinel = SUB_BUCKETS * token_total
    source_list = []
    slot_list = []
    key_list = []
    for turn_index in range(ROUNDS):
        target = groups[turn_index, :, 0]
        one_hot = (target[:, None] == jnp.arange(seq_count, dtype=jnp.int32)[None, :]).astype(
            jnp.int32
        )
        dest_rank = jnp.sum(jnp.cumsum(one_hot, axis=0) * one_hot, axis=1) - 1
        slot_index = target * capacity + dest_rank
        source_list.append(
            jnp.full((slot_count,), tokens_here, jnp.int32)
            .at[slot_index]
            .set(jnp.arange(tokens_here, dtype=jnp.int32))
        )
        slot_list.append(slot_index)
        sort_keys = (
            jnp.full((slot_count,), sentinel, jnp.int32)
            .at[slot_index]
            .set(buckets[turn_index] * token_total + position)
        )
        key_list.append(sort_keys.reshape(seq_count, capacity))
    arrived_keys = lax.all_to_all(
        jnp.stack(key_list, axis=1), "seq", split_axis=0, concat_axis=0, tiled=True
    )
    orderings = []
    inverses = []
    live_list = []
    for turn_index in range(ROUNDS):
        received = arrived_keys[:, turn_index].reshape(slot_count)
        ordering = jnp.argsort(received, stable=True)
        orderings.append(ordering)
        inverses.append(jnp.argsort(ordering))
        live_list.append(received[ordering] < sentinel)

    def pack_rows(token_rows):
        return jnp.stack(
            [
                spread_rows(token_rows, source_list[turn_index]).reshape(
                    (seq_count, capacity) + token_rows.shape[1:]
                )
                for turn_index in range(ROUNDS)
            ],
            axis=1,
        )

    def sorted_rows(buffer, turn_index):
        return buffer[:, turn_index].reshape((slot_count,) + buffer.shape[3:])[
            orderings[turn_index]
        ]

    def unsorted(token_rows, turn_index):
        return token_rows[inverses[turn_index]].reshape(
            (seq_count, capacity) + token_rows.shape[1:]
        )

    def home_rows(buffer, turn_index):
        return buffer[:, turn_index].reshape((slot_count,) + buffer.shape[3:])[
            slot_list[turn_index]
        ]

    query_buffer = pack_rows(queries)
    value_buffer = pack_rows(values)
    got_queries, got_values = (
        lax.all_to_all(query_buffer, "seq", split_axis=0, concat_axis=0, tiled=True),
        lax.all_to_all(value_buffer, "seq", split_axis=0, concat_axis=0, tiled=True),
    )
    mixed_list = []
    log_list = []
    for turn_index in range(ROUNDS):
        mixed_rows, log_total = forward_rows(
            sorted_rows(got_queries, turn_index),
            sorted_rows(got_values, turn_index),
            live_list[turn_index],
        )
        mixed_list.append(unsorted(mixed_rows, turn_index))
        log_list.append(unsorted(log_total, turn_index))
    back_mixed, back_logs = (
        lax.all_to_all(
            jnp.stack(mixed_list, axis=1), "seq", split_axis=0, concat_axis=0, tiled=True
        ),
        lax.all_to_all(jnp.stack(log_list, axis=1), "seq", split_axis=0, concat_axis=0, tiled=True),
    )
    turn_mixed = jnp.stack([home_rows(back_mixed, turn_index) for turn_index in range(ROUNDS)])
    turn_logs = jnp.stack([home_rows(back_logs, turn_index) for turn_index in range(ROUNDS)])
    largest = jnp.max(turn_logs, axis=0)
    log_all = largest + jnp.log(jnp.sum(jnp.exp(turn_logs - largest), axis=0))
    mix_weights = jnp.exp(turn_logs - log_all)
    combined = jnp.sum(mix_weights[..., None] * turn_mixed, axis=0)
    output = combined.reshape(tokens_here, width_here).astype(jnp.bfloat16)
    out_grads = out_cotangent.reshape(tokens_here, heads_here, HEAD_DIM)
    out_inner = jnp.sum(out_grads.astype(jnp.float32) * combined, axis=-1)
    weight_buffer = jnp.stack(
        [
            spread_rows(mix_weights[turn_index], source_list[turn_index]).reshape(
                seq_count, capacity, heads_here
            )
            for turn_index in range(ROUNDS)
        ],
        axis=1,
    )
    inner_buffer = pack_rows(out_inner)
    got_mixes, got_inners = (
        lax.all_to_all(weight_buffer, "seq", split_axis=0, concat_axis=0, tiled=True),
        lax.all_to_all(inner_buffer, "seq", split_axis=0, concat_axis=0, tiled=True),
    )
    grad_buffer = pack_rows(out_grads)
    back_queries, back_values, got_grads = (
        lax.all_to_all(query_buffer, "seq", split_axis=0, concat_axis=0, tiled=True),
        lax.all_to_all(value_buffer, "seq", split_axis=0, concat_axis=0, tiled=True),
        lax.all_to_all(grad_buffer, "seq", split_axis=0, concat_axis=0, tiled=True),
    )
    query_list = []
    value_list = []
    for turn_index in range(ROUNDS):
        query_turn, value_turn = backward_rows(
            sorted_rows(back_queries, turn_index),
            sorted_rows(back_values, turn_index),
            live_list[turn_index],
            sorted_rows(got_grads, turn_index),
            sorted_rows(got_mixes, turn_index),
            sorted_rows(got_inners, turn_index),
        )
        query_list.append(unsorted(query_turn, turn_index))
        value_list.append(unsorted(value_turn, turn_index))
    back_query, back_value = (
        lax.all_to_all(
            jnp.stack(query_list, axis=1), "seq", split_axis=0, concat_axis=0, tiled=True
        ),
        lax.all_to_all(
            jnp.stack(value_list, axis=1), "seq", split_axis=0, concat_axis=0, tiled=True
        ),
    )
    query_sum = home_rows(back_query, 0).astype(jnp.float32)
    value_sum = home_rows(back_value, 0).astype(jnp.float32)
    turn_index = 1
    query_sum = query_sum + home_rows(back_query, turn_index).astype(jnp.float32)
    value_sum = value_sum + home_rows(back_value, turn_index).astype(jnp.float32)
    query_grad = query_sum.reshape(tokens_here, width_here).astype(jnp.bfloat16)
    value_grad = value_sum.reshape(tokens_here, width_here).astype(jnp.bfloat16)
    contract_cols = (((1,), (1,)), ((), ()))
    terms = lax.dot_general(
        query_grad, full_weights[0], contract_cols, preferred_element_type=jnp.float32
    ) + lax.dot_general(
        value_grad, full_weights[1], contract_cols, preferred_element_type=jnp.float32
    )
    input_grad = lax.psum_scatter(
        terms.astype(jnp.bfloat16), "head", scatter_dimension=1, tiled=True
    )
    contract_rows = (((0,), (0,)), ((), ()))
    query_part = lax.dot_general(
        features, query_grad, contract_rows, preferred_element_type=jnp.float32
    )
    value_part = lax.dot_general(
        features, value_grad, contract_rows, preferred_element_type=jnp.float32
    )
    weight_grads = lax.psum_scatter(
        jnp.stack((query_part, value_part), axis=1).astype(jnp.bfloat16),
        "seq",
        scatter_dimension=0,
        tiled=True,
    ).astype(jnp.float32)
    return (output, input_grad, weight_grads[:, 0], weight_grads[:, 1])


def solution(mesh):
    return jax.shard_map(
        per_device,
        mesh=mesh,
        in_specs=(
            P("seq", "head"),
            P("seq", "head"),
            P("seq", "head"),
            P(None, "seq", None),
            P(None, "seq"),
            P("seq", "head"),
        ),
        out_specs=(P("seq", "head"), P("seq", "head"), P("seq", "head"), P("seq", "head")),
        check_vma=False,
    )
```

profile of v0, /device:TPU:8, one launch (start us, length us, event | category | flops | bytes accessed | tf_op | source)
XLA Modules:
  0.0 559.9 jit_solution(9881908167255207444)
XLA Ops:
  19.6 7.4 %all-to-all-start = ((s32[16,2,48]{2,1,0:T(2,128)}), s32[16,2,48]{2,1,0:T(2,128)S(1)}, u32[]{:S(2)}, u32[]{:S(2)}) async-start(s32[16,2,48]{2,1,0:T(2,128)} %pad_add_fusion), calls=%async_computation | async-start | bytes 32768 | tf_op jit(solution)/shard_map/all_to_all | solution.py:161
  29.5 2.9 scatter_custom_fusion.2
  32.7 2.9 gather_fusion.22
  35.6 2.9 gather_fusion.21
  42.5 4.4 sort.64
  46.9 3.2 gather_fusion.5
  50.1 4.4 sort.65
  54.4 4.4 sort.62
  58.8 3.2 gather_fusion
  62.1 64.8 %all-gather.3.cloned.1.call-done = bf16[2,4096,256]{1,2,0:T(8,128)(2,1)} async-done(((bf16[2,256,256]{1,2,0:T(8,128)(2,1)}), bf16[2,4096,256]{1,2,0:T(8,128)(2,1)}) %all-gather.3.cloned.1.call-update) | async-done | bytes 4194320 | tf_op jit(solution)/shard_map/all_gather | solution.py:131
  126.9 5.8 %fusion.12 = bf16[512,2,256]{0,2,1:T(8,128)(2,1)S(1)} fusion(bf16[2,4096,256]{1,2,0:T(8,128)(2,1)} %all-gather.3.cloned.1.call-done, bf16[512,4096]{1,0:T(8,128)(2,1)} %all-gather.5.cloned.1.call-done), kind=kOutput, calls=%fused_computation.75 | convolution fusion | flops 2147745792 | bytes 8912896 | tf_op jit(solution)/shard_map/td,kdc->tkc/dot_general | solution.py:132
  133.2 2.9 gather_fusion.2
  136.1 2.9 gather_fusion.1
  140.2 5.8 %all-to-all-start.1 = ((bf16[16,2,48,2,128]{4,2,3,1,0:T(8,128)(2,1)}), bf16[16,2,48,2,128]{4,2,3,1,0:T(8,128)(2,1)S(1)}, u32[]{:S(2)}, u32[]{:S(2)}) async-start(bf16[16,2,48,2,128]{4,2,3,1,0:T(8,128)(2,1)} %copy.474), calls=%async_computation.1 | async-start | bytes 1572864 | tf_op jit(solution)/shard_map/all_to_all | solution.py:203
  146.5 4.4 sort.63
  152.5 2.9 gather_fusion.11
  155.4 2.9 gather_fusion.10
  159.6 7.5 %all-to-all-start.3 = ((bf16[16,2,48,2,128]{4,2,3,1,0:T(8,128)(2,1)}), bf16[16,2,48,2,128]{4,2,3,1,0:T(8,128)(2,1)S(1)}, u32[]{:S(2)}, u32[]{:S(2)}) async-start(bf16[16,2,48,2,128]{4,2,3,1,0:T(8,128)(2,1)} %copy.507), calls=%async_computation.3 | async-start | bytes 1572864 | tf_op jit(solution)/shard_map/all_to_all | solution.py:204
  167.6 2.9 gather_fusion.3
  172.4 2.9 gather_fusion.6
  179.0 2.9 gather_fusion.12
  182.6 2.9 gather_fusion.14
  204.8 7.2 %all-to-all-start.2 = ((f32[16,1,192]{2,1,0:T(1,128)}), f32[16,1,192]{2,1,0:T(1,128)}, u32[]{:S(2)}, u32[]{:S(2)}) async-start(f32[16,1,192]{2,1,0:T(1,128)} %reshape.780), calls=%async_computation.2 | async-start | bytes 32768 | tf_op jit(solution)/shard_map/all_to_all | solution.py:220
  216.7 3.2 gather_fusion.15
  220.7 3.2 gather_fusion.13
  223.9 7.2 %all-to-all-start.6 = ((bf16[16,2,48,2,128]{4,3,2,1,0:T(2,128)(2,1)}), bf16[16,2,48,2,128]{4,3,2,1,0:T(2,128)(2,1)S(1)}, u32[]{:S(2)}, u32[]{:S(2)}) async-start(bf16[16,2,48,2,128]{4,3,2,1,0:T(2,128)(2,1)} %pad_maximum_fusion.4), calls=%async_computation.6 | async-start | bytes 1572864 | tf_op jit(solution)/shard_map/all_to_all | solution.py:249
  245.4 7.2 %all-to-all-start.5 = ((f32[16,1,192]{2,1,0:T(1,128)}), f32[16,1,192]{2,1,0:T(1,128)S(1)}, u32[]{:S(2)}, u32[]{:S(2)}) async-start(f32[16,1,192]{2,1,0:T(1,128)} %reshape.784), calls=%async_computation.5 | async-start | bytes 32768 | tf_op jit(solution)/shard_map/all_to_all | solution.py:242
  252.6 3.3 pad_maximum_fusion.1
  255.9 3.0 all-to-all-done.5
  259.5 5.0 all-to-all-start.4
  267.0 2.8 gather_fusion.23
  270.5 2.8 gather_fusion.29
  297.1 3.5 gather_fusion.35
  305.2 3.6 gather_fusion.34
  315.5 3.1 fusion.15
  324.5 7.3 %all-to-all-start.7 = ((f32[16,1,192]{2,1,0:T(1,128)}), f32[16,1,192]{2,1,0:T(1,128)S(1)}, u32[]{:S(2)}, u32[]{:S(2)}) async-start(f32[16,1,192]{2,1,0:T(1,128)} %reshape.782), calls=%async_computation.7 | async-start | bytes 32768 | tf_op jit(solution)/shard_map/all_to_all | solution.py:243
  333.7 4.3 all-to-all-done.7
  338.0 5.8 %all-to-all-start.9 = ((bf16[16,2,48,2,128]{4,3,2,1,0:T(2,128)(2,1)}), bf16[16,2,48,2,128]{4,3,2,1,0:T(2,128)(2,1)}, u32[]{:S(2)}, u32[]{:S(2)}) async-start(bf16[16,2,48,2,128]{4,3,2,1,0:T(2,128)(2,1)} %pad_maximum_fusion.6), calls=%async_computation.9 | async-start | bytes 1572864 | tf_op jit(solution)/shard_map/all_to_all | solution.py:268
  357.5 2.8 select_convert_fusion.1
  365.8 2.9 gather_fusion.27
  369.7 2.9 gather_fusion.31
  374.6 7.3 %all-to-all-start.8 = ((bf16[16,2,48,2,128]{4,3,2,1,0:T(2,128)(2,1)}), bf16[16,2,48,2,128]{4,3,2,1,0:T(2,128)(2,1)S(1)}, u32[]{:S(2)}, u32[]{:S(2)}) async-start(bf16[16,2,48,2,128]{4,3,2,1,0:T(2,128)(2,1)} %pad_maximum_fusion.5), calls=%async_computation.8 | async-start | bytes 1572864 | tf_op jit(solution)/shard_map/all_to_all | solution.py:265
  388.3 3.4 fusion.1
  398.0 3.4 fusion
  403.9 3.0 fusion.4
  406.9 3.3 add_convert_fusion
  411.9 75.5 %reduce-scatter.5.cloned.1.call-done = bf16[256,2,256]{0,2,1:T(8,128)(2,1)} async-done(((bf16[4096,2,256]{0,2,1:T(8,128)(2,1)}), bf16[256,2,256]{0,2,1:T(8,128)(2,1)}) %reduce-scatter.5.cloned.1.call-update) | async-done | bytes 262160 | tf_op jit(solution)/shard_map/reduce_scatter | solution.py:295
  490.1 63.1 %reduce-scatter.3.cloned.1.call-done = bf16[512,256]{1,0:T(8,128)(2,1)} async-done(((bf16[512,4096]{1,0:T(8,128)(2,1)}), bf16[512,256]{1,0:T(8,128)(2,1)}) %reduce-scatter.3.cloned.1.call-update) | async-done | bytes 262160 | tf_op jit(solution)/shard_map/reduce_scatter | solution.py:285
  (408 shorter events, 157.0 us)
Async XLA Ops:
  7.2 3.6 copy-start.70
  7.2 6.7 %copy-start.73 = (s32[2,512]{1,0:T(2,128)S(1)}, s32[2,512]{1,0:T(2,128)}, u32[]{:S(2)}) copy-start(s32[2,512]{1,0:T(2,128)} %param.10) | copy-start | bytes 12292
  7.2 25.2 %copy-start.33 = (bf16[512,256]{1,0:T(8,128)(2,1)S(1)}, bf16[512,256]{1,0:T(8,128)(2,1)}, u32[]{:S(2)}) copy-start(bf16[512,256]{1,0:T(8,128)(2,1)} %param.11) | copy-start | bytes 786436
  7.2 54.9 %all-gather.5.cloned.1.call-start = ((), (), s32[]{:S(2)}) async-start(), calls=%async_computation.13 | async-start | bytes 4456448 | tf_op jit(solution)/shard_map/all_gather | solution.py:129
  7.9 119.0 %all-gather.3.cloned.1.call-start = ((), (), s32[]{:S(2)}) async-start(), calls=%async_computation.12 | async-start | bytes 4456448 | tf_op jit(solution)/shard_map/all_gather | solution.py:131
  19.6 22.7 %all-to-all-start = ((s32[16,2,48]{2,1,0:T(2,128)}), s32[16,2,48]{2,1,0:T(2,128)S(1)}, u32[]{:S(2)}, u32[]{:S(2)}) async-start(s32[16,2,48]{2,1,0:T(2,128)} %pad_add_fusion), calls=%async_computation | async-start | bytes 32768 | tf_op jit(solution)/shard_map/all_to_all | solution.py:161
  32.5 9.2 %copy-start.8 = (bf16[512,2,128]{2,1,0:T(2,128)(2,1)}, bf16[512,2,128]{2,1,0:T(2,128)(2,1)S(1)}, u32[]{:S(2)}) copy-start(bf16[512,2,128]{2,1,0:T(2,128)(2,1)S(1)} %reshape.381) | copy-start | bytes 786436
  35.6 119.8 %copy-start.34 = (s32[1024]{0:T(1024)}, s32[1024]{0:T(1024)S(1)}, u32[]{:S(2)}) copy-start(s32[1024]{0:T(1024)S(1)} %pad_clamp_fusion.6) | copy-start | bytes 12292
  140.2 19.4 %all-to-all-start.1 = ((bf16[16,2,48,2,128]{4,2,3,1,0:T(8,128)(2,1)}), bf16[16,2,48,2,128]{4,2,3,1,0:T(8,128)(2,1)S(1)}, u32[]{:S(2)}, u32[]{:S(2)}) async-start(bf16[16,2,48,2,128]{4,2,3,1,0:T(8,128)(2,1)} %copy.474), calls=%async_computation.1 | async-start | bytes 1572864 | tf_op jit(solution)/shard_map/all_to_all | solution.py:203
  151.5 65.2 %copy-start.36 = (s32[1024]{0:T(1024)}, s32[1024]{0:T(1024)S(1)}, u32[]{:S(2)}) copy-start(s32[1024]{0:T(1024)S(1)} %pad_clamp_fusion.2) | copy-start | bytes 12292
  159.6 18.9 %all-to-all-start.3 = ((bf16[16,2,48,2,128]{4,2,3,1,0:T(8,128)(2,1)}), bf16[16,2,48,2,128]{4,2,3,1,0:T(8,128)(2,1)S(1)}, u32[]{:S(2)}, u32[]{:S(2)}) async-start(bf16[16,2,48,2,128]{4,2,3,1,0:T(8,128)(2,1)} %copy.507), calls=%async_computation.3 | async-start | bytes 1572864 | tf_op jit(solution)/shard_map/all_to_all | solution.py:204
  177.4 13.2 %copy-start.29 = (bf16[640,2,128]{2,0,1:T(8,128)(2,1)}, bf16[640,2,128]{2,0,1:T(8,128)(2,1)S(1)}, u32[]{:S(2)}) copy-start(bf16[640,2,128]{2,0,1:T(8,128)(2,1)S(1)} %slice.414) | copy-start | bytes 983044
  178.1 12.5 %copy-start.40 = (bf16[1,128,2,128]{3,1,2,0:T(8,128)(2,1)}, bf16[1,128,2,128]{3,1,2,0:T(8,128)(2,1)S(1)}, u32[]{:S(2)}) copy-start(bf16[1,128,2,128]{3,1,2,0:T(8,128)(2,1)S(1)} %slice_bitcast_fusion.8) | copy-start | bytes 196612
  185.8 4.5 copy-start.69
  187.2 3.4 copy-start.60
  187.2 3.4 copy-start.74
  191.3 2.9 copy-start.66
  197.0 17.4 %copy-start.10 = (f32[6,2,128,256]{3,2,1,0:T(8,128)}, f32[6,2,128,256]{3,2,1,0:T(8,128)S(1)}, u32[]{:S(2)}) copy-start(f32[6,2,128,256]{3,2,1,0:T(8,128)S(1)} %get-tuple-element.85) | copy-start | bytes 4718596
  204.8 19.2 %all-to-all-start.2 = ((f32[16,1,192]{2,1,0:T(1,128)}), f32[16,1,192]{2,1,0:T(1,128)}, u32[]{:S(2)}, u32[]{:S(2)}) async-start(f32[16,1,192]{2,1,0:T(1,128)} %reshape.780), calls=%async_computation.2 | async-start | bytes 32768 | tf_op jit(solution)/shard_map/all_to_all | solution.py:220
  216.1 3.9 copy-start.19
  220.7 12.8 %copy-start.54 = (s32[1024]{0:T(1024)S(1)}, s32[1024]{0:T(1024)}, u32[]{:S(2)}) copy-start(s32[1024]{0:T(1024)} %pad_clamp_fusion) | copy-start | bytes 12292
  223.9 21.5 %all-to-all-start.6 = ((bf16[16,2,48,2,128]{4,3,2,1,0:T(2,128)(2,1)}), bf16[16,2,48,2,128]{4,3,2,1,0:T(2,128)(2,1)S(1)}, u32[]{:S(2)}, u32[]{:S(2)}) async-start(bf16[16,2,48,2,128]{4,3,2,1,0:T(2,128)(2,1)} %pad_maximum_fusion.4), calls=%async_computation.6 | async-start | bytes 1572864 | tf_op jit(solution)/shard_map/all_to_all | solution.py:249
  241.2 3.5 copy-start.45
  241.2 11.5 %copy-start.4 = (f32[768,2,128]{2,1,0:T(2,128)S(1)}, f32[768,2,128]{2,1,0:T(2,128)}, u32[]{:S(2)}) copy-start(f32[768,2,128]{2,1,0:T(2,128)} %gather_fusion.15) | copy-start | bytes 2359300
  245.4 10.5 %copy-start.3 = (bf16[16,2,48,2,128]{4,3,2,1,0:T(2,128)(2,1)}, bf16[16,2,48,2,128]{4,3,2,1,0:T(2,128)(2,1)S(1)}, u32[]{:S(2)}) copy-start(bf16[16,2,48,2,128]{4,3,2,1,0:T(2,128)(2,1)S(1)} %all-to-all-done.6) | copy-start | bytes 2359300
  245.4 13.5 %all-to-all-start.5 = ((f32[16,1,192]{2,1,0:T(1,128)}), f32[16,1,192]{2,1,0:T(1,128)S(1)}, u32[]{:S(2)}, u32[]{:S(2)}) async-start(f32[16,1,192]{2,1,0:T(1,128)} %reshape.784), calls=%async_computation.5 | async-start | bytes 32768 | tf_op jit(solution)/shard_map/all_to_all | solution.py:242
  259.5 49.4 %all-to-all-start.4 = ((f32[16,2,48,2,128]{4,3,2,1,0:T(2,128)}), f32[16,2,48,2,128]{4,3,2,1,0:T(2,128)S(1)}, u32[]{:S(2)}, u32[]{:S(2)}) async-start(f32[16,2,48,2,128]{4,3,2,1,0:T(2,128)} %pad_maximum_fusion.1), calls=%async_computation.4 | async-start | bytes 3145728 | tf_op jit(solution)/shard_map/all_to_all | solution.py:217
  289.5 4.2 copy-start.14
  293.8 3.3 copy-start.37
  308.8 4.0 copy-start.55
  310.2 5.4 copy-start.1
  312.9 5.8 %copy-start.9 = (bf16[512,2,128]{2,1,0:T(2,128)(2,1)S(1)}, bf16[512,2,128]{2,1,0:T(2,128)(2,1)}, u32[]{:S(2)}) copy-start(bf16[512,2,128]{2,1,0:T(2,128)(2,1)} %copy-done.8) | copy-start | bytes 786436
  321.8 10.0 %copy-start.16 = (bf16[768,2,128]{2,1,0:T(2,128)(2,1)S(1)}, bf16[768,2,128]{2,1,0:T(2,128)(2,1)}, u32[]{:S(2)}) copy-start(bf16[768,2,128]{2,1,0:T(2,128)(2,1)} %gather_fusion.35) | copy-start | bytes 1179652
  321.8 10.0 %copy-start.17 = (bf16[768,2,128]{2,1,0:T(2,128)(2,1)S(1)}, bf16[768,2,128]{2,1,0:T(2,128)(2,1)}, u32[]{:S(2)}) copy-start(bf16[768,2,128]{2,1,0:T(2,128)(2,1)} %gather_fusion.34) | copy-start | bytes 1179652
  324.5 13.5 %all-to-all-start.7 = ((f32[16,1,192]{2,1,0:T(1,128)}), f32[16,1,192]{2,1,0:T(1,128)S(1)}, u32[]{:S(2)}, u32[]{:S(2)}) async-start(f32[16,1,192]{2,1,0:T(1,128)} %reshape.782), calls=%async_computation.7 | async-start | bytes 32768 | tf_op jit(solution)/shard_map/all_to_all | solution.py:243
  338.0 36.6 %all-to-all-start.9 = ((bf16[16,2,48,2,128]{4,3,2,1,0:T(2,128)(2,1)}), bf16[16,2,48,2,128]{4,3,2,1,0:T(2,128)(2,1)}, u32[]{:S(2)}, u32[]{:S(2)}) async-start(bf16[16,2,48,2,128]{4,3,2,1,0:T(2,128)(2,1)} %pad_maximum_fusion.6), calls=%async_computation.9 | async-start | bytes 1572864 | tf_op jit(solution)/shard_map/all_to_all | solution.py:268
  345.5 3.4 copy-start.12
  354.0 3.4 copy-start.63
  357.4 2.8 copy-start.31
  365.1 3.6 copy-start.5
  365.2 3.6 copy-start.51
  365.2 3.6 copy-start.47
  374.6 9.0 %copy-start.59 = (s32[1024]{0:T(1024)S(1)}, s32[1024]{0:T(1024)}, u32[]{:S(2)}) copy-start(s32[1024]{0:T(1024)} %pad_clamp_fusion.1) | copy-start | bytes 12292
  374.6 11.4 %copy-start.56 = (s32[1024]{0:T(1024)S(1)}, s32[1024]{0:T(1024)}, u32[]{:S(2)}) copy-start(s32[1024]{0:T(1024)} %pad_clamp_fusion) | copy-start | bytes 12292
  374.6 17.4 %all-to-all-start.8 = ((bf16[16,2,48,2,128]{4,3,2,1,0:T(2,128)(2,1)}), bf16[16,2,48,2,128]{4,3,2,1,0:T(2,128)(2,1)S(1)}, u32[]{:S(2)}, u32[]{:S(2)}) async-start(bf16[16,2,48,2,128]{4,3,2,1,0:T(2,128)(2,1)} %pad_maximum_fusion.5), calls=%async_computation.8 | async-start | bytes 1572864 | tf_op jit(solution)/shard_map/all_to_all | solution.py:265
  381.9 105.5 %reduce-scatter.5.cloned.1.call-start = ((), (), s32[]{:S(2)}) async-start(), calls=%async_computation.15 | async-start | bytes 4456448 | tf_op jit(solution)/shard_map/reduce_scatter | solution.py:295
  403.8 149.3 %reduce-scatter.3.cloned.1.call-start = ((), (), s32[]{:S(2)}) async-start(), calls=%async_computation.14 | async-start | bytes 4456448 | tf_op jit(solution)/shard_map/reduce_scatter | solution.py:285
  403.9 3.0 copy-start.2
  (41 other events, 63.5 us)
Sparse Core Ops, SparseCore 0:
  9.8 51.8 all-gather.4
  64.7 62.1 all-gather.2
  404.0 83.3 reduce-scatter.4
  490.5 62.5 reduce-scatter.2
where the time goes:
time: 567 us; the launch traced here: 560 us
  waiting for transfers between devices  212 us (37%)
  local copies, waits for them, and re-layouts  171 us (30%)
  starting transfers between devices  67.8 us (12%)
  other arithmetic  56.9 us (10%)
  matrix products  36.6 us (6%)
  between operations  16 us (3%)
    reduce_scatter x1, waiting for transfers between devices, per_device(): lax.psum_scatter(jnp.stack((query_part, value_part), axis=1).astype(jnp.b...  75.5 us
    all_gather x1, waiting for transfers between devices, per_device(): full_weights = lax.all_gather(stacked, 'seq', axis=1, tiled=True)  64.8 us
    reduce_scatter x1, waiting for transfers between devices, per_device(): lax.psum_scatter(terms.astype(jnp.bfloat16), 'head', scatter_dimension=1,...  63.1 us
    gather x14, local copies, waits for them, and re-layouts, sorted_rows(): buffer[:, turn_index].reshape((slot_count,) + buffer.shape[3:])  28.3 us
    gather x14, local copies, waits for them, and re-layouts, spread_rows(): return padded[source_rows]  24.8 us
    gather x8, local copies, waits for them, and re-layouts, unsorted(): token_rows[inverses[turn_index]]  23.4 us
    gather x10, local copies, waits for them, and re-layouts, home_rows(): buffer[:, turn_index].reshape((slot_count,) + buffer.shape[3:])  16.5 us
    unnamed x167, local copies, waits for them, and re-layouts  13.6 us
  transfers between devices with their start and end apart: 14, of which 7 were waited for; matrix products, arithmetic and copies ran while one was open for 35% of the time, Pallas kernels for 0%

commit v1 on v0

--- a/solution.py
+++ b/solution.py
@@ -128,7 +128,12 @@
     slot_count = seq_count * capacity
     features = lax.all_gather(layer_input, "head", axis=1, tiled=True)
     stacked = jnp.stack((qk_weight, value_weight))
-    full_weights = lax.all_gather(stacked, "seq", axis=1, tiled=True)
+    sides = []
+    for _ in range(lax.axis_size("seq")):
+        sides.append(stacked)
+    full_weights = jnp.concatenate(
+        lax.all_to_all(jnp.stack(sides), split_axis=0, concat_axis=0, axis_name="seq"), axis=1
+    )
     projected = jnp.einsum(
         "td,kdc->tkc", features, full_weights, preferred_element_type=jnp.float32
     )

time: 567 us -> 549 us (0.968)
  waiting for transfers between devices: 212 us -> 165 us
  local copies, waits for them, and re-layouts: 171 us -> 185 us
  starting transfers between devices: 67.8 us -> 81.6 us
    all_gather x1 -> x0, waiting for transfers between devices: 64.8 us -> none  [per_device(): full_weights = lax.all_gather(stacked, 'seq', axis=1, tiled=True)]
    all_to_all x0 -> x1, waiting for transfers between devices: none -> 23.6 us  [per_device(): lax.all_to_all(jnp.stack(sides), split_axis=0, concat_axis=0, axis_name='...]
    all_to_all x0 -> x1, starting transfers between devices: none -> 7.84 us  [per_device(): lax.all_to_all(jnp.stack(sides), split_axis=0, concat_axis=0, axis_name='...]
    all_to_all x0 -> x1, local copies, waits for them, and re-layouts: none -> 6.28 us  [per_device(): lax.all_to_all(jnp.stack(sides), split_axis=0, concat_axis=0, axis_name='...]
    all_to_all x1, starting transfers between devices: 5.76 us -> 11.4 us  [per_device(): lax.all_to_all(query_buffer, 'seq', split_axis=0, concat_axis=0, tiled=True)]
    unnamed x167 -> x153, local copies, waits for them, and re-layouts: 13.6 us -> 11.6 us
  transfers between devices with their start and end apart: 14 -> 14, of which waited for: 7 -> 6; matrix products, arithmetic and copies ran while one was open for 35% -> 39% of each run, Pallas kernels for 0% -> 0%
where the time goes in v1:
time: 549 us; the launch traced here: 541 us
  local copies, waits for them, and re-layouts  185 us (34%)
  waiting for transfers between devices  165 us (30%)
  starting transfers between devices  81.6 us (15%)
  other arithmetic  58.9 us (11%)
  matrix products  34.9 us (6%)
  between operations  15.8 us (3%)
    reduce_scatter x1, waiting for transfers between devices, per_device(): lax.psum_scatter(jnp.stack((query_part, value_part), axis=1).astype(jnp.b...  70 us
    reduce_scatter x1, waiting for transfers between devices, per_device(): lax.psum_scatter(terms.astype(jnp.bfloat16), 'head', scatter_dimension=1,...  63.1 us
    gather x14, local copies, waits for them, and re-layouts, sorted_rows(): buffer[:, turn_index].reshape((slot_count,) + buffer.shape[3:])  28.3 us
    gather x14, local copies, waits for them, and re-layouts, spread_rows(): return padded[source_rows]  24.1 us
    all_to_all x1, waiting for transfers between devices, per_device(): lax.all_to_all(jnp.stack(sides), split_axis=0, concat_axis=0, axis_name='...  23.6 us
    gather x8, local copies, waits for them, and re-layouts, unsorted(): token_rows[inverses[turn_index]]  23.4 us
    gather x10, local copies, waits for them, and re-layouts, home_rows(): buffer[:, turn_index].reshape((slot_count,) + buffer.shape[3:])  16.5 us
    unnamed x153, local copies, waits for them, and re-layouts  11.6 us
  transfers between devices with their start and end apart: 14, of which 6 were waited for; matrix products, arithmetic and copies ran while one was open for 39% of the time, Pallas kernels for 0%

profile of v1, /device:TPU:8, one launch (start us, length us, event | category | flops | bytes accessed | tf_op | source)
XLA Modules:
  0.0 541.4 jit_solution(11178350300973509998)
XLA Ops:
  18.9 7.4 %all-to-all-start = ((s32[16,2,48]{2,1,0:T(2,128)}), s32[16,2,48]{2,1,0:T(2,128)S(1)}, u32[]{:S(2)}, u32[]{:S(2)}) async-start(s32[16,2,48]{2,1,0:T(2,128)} %pad_add_fusion), calls=%async_computation | async-start | bytes 32768 | tf_op jit(solution)/shard_map/all_to_all | solution.py:166
  36.0 7.8 %all-to-all-start.1 = ((bf16[16,2,256,256]{2,3,1,0:T(8,128)(2,1)}), bf16[16,2,256,256]{2,3,1,0:T(8,128)(2,1)}, u32[]{:S(2)}, u32[]{:S(2)}) async-start(bf16[16,2,256,256]{2,3,1,0:T(8,128)(2,1)} %stack.92), calls=%async_computation.1 | async-start | bytes 8388608 | tf_op jit(solution)/shard_map/all_to_all | solution.py:135
  43.9 2.9 gather_fusion.22
  46.8 2.9 gather_fusion.21
  53.7 4.4 sort.64
  58.1 3.2 gather_fusion.5
  61.3 4.4 sort.65
  65.6 4.4 sort.62
  70.0 3.2 gather_fusion
  73.3 23.6 %all-to-all-done.1 = bf16[16,2,256,256]{2,3,1,0:T(8,128)(2,1)} async-done(((bf16[16,2,256,256]{2,3,1,0:T(8,128)(2,1)}), bf16[16,2,256,256]{2,3,1,0:T(8,128)(2,1)}, u32[]{:S(2)}, u32[]{:S(2)}) %all-to-all-start.1) | async-done | bytes 4194336 | tf_op jit(solution)/shard_map/all_to_all | solution.py:135
  96.9 4.7 copy.703
  101.7 5.8 %fusion.11 = bf16[512,2,256]{0,2,1:T(8,128)(2,1)S(1)} fusion(bf16[2,4096,256]{1,2,0:T(8,128)(2,1)} %bitcast.276, bf16[512,4096]{1,0:T(8,128)(2,1)} %all-gather.2.cloned.1.call-done), kind=kOutput, calls=%fused_computation.72 | convolution fusion | flops 2147745792 | bytes 8912896 | tf_op jit(solution)/shard_map/td,kdc->tkc/dot_general | solution.py:137
  107.9 2.9 gather_fusion.2
  110.8 2.9 gather_fusion.1
  114.9 11.4 %all-to-all-start.2 = ((bf16[16,2,48,2,128]{4,2,3,1,0:T(8,128)(2,1)}), bf16[16,2,48,2,128]{4,2,3,1,0:T(8,128)(2,1)S(1)}, u32[]{:S(2)}, u32[]{:S(2)}) async-start(bf16[16,2,48,2,128]{4,2,3,1,0:T(8,128)(2,1)} %copy.577), calls=%async_computation.2 | async-start | bytes 1572864 | tf_op jit(solution)/shard_map/all_to_all | solution.py:208
  126.9 4.4 sort.63
  132.9 2.9 gather_fusion.11
  135.8 2.9 gather_fusion.10
  139.9 7.5 %all-to-all-start.4 = ((bf16[16,2,48,2,128]{4,2,3,1,0:T(8,128)(2,1)}), bf16[16,2,48,2,128]{4,2,3,1,0:T(8,128)(2,1)S(1)}, u32[]{:S(2)}, u32[]{:S(2)}) async-start(bf16[16,2,48,2,128]{4,2,3,1,0:T(8,128)(2,1)} %copy.610), calls=%async_computation.4 | async-start | bytes 1572864 | tf_op jit(solution)/shard_map/all_to_all | solution.py:209
  147.9 2.9 gather_fusion.3
  152.7 2.9 gather_fusion.6
  158.9 2.9 gather_fusion.12
  162.6 2.9 gather_fusion.14
  184.7 7.6 %all-to-all-start.3 = ((f32[16,1,192]{2,1,0:T(1,128)}), f32[16,1,192]{2,1,0:T(1,128)}, u32[]{:S(2)}, u32[]{:S(2)}) async-start(f32[16,1,192]{2,1,0:T(1,128)} %reshape.794), calls=%async_computation.3 | async-start | bytes 32768 | tf_op jit(solution)/shard_map/all_to_all | solution.py:225
  197.0 3.2 gather_fusion.15
  200.9 3.2 gather_fusion.13
  204.2 7.2 %all-to-all-start.7 = ((bf16[16,2,48,2,128]{4,3,2,1,0:T(2,128)(2,1)}), bf16[16,2,48,2,128]{4,3,2,1,0:T(2,128)(2,1)S(1)}, u32[]{:S(2)}, u32[]{:S(2)}) async-start(bf16[16,2,48,2,128]{4,3,2,1,0:T(2,128)(2,1)} %pad_maximum_fusion.4), calls=%async_computation.7 | async-start | bytes 1572864 | tf_op jit(solution)/shard_map/all_to_all | solution.py:254
  225.2 7.2 %all-to-all-start.6 = ((f32[16,1,192]{2,1,0:T(1,128)}), f32[16,1,192]{2,1,0:T(1,128)S(1)}, u32[]{:S(2)}, u32[]{:S(2)}) async-start(f32[16,1,192]{2,1,0:T(1,128)} %reshape.798), calls=%async_computation.6 | async-start | bytes 32768 | tf_op jit(solution)/shard_map/all_to_all | solution.py:247
  232.4 3.5 pad_maximum_fusion.1
  239.3 5.0 all-to-all-start.5
  246.8 2.8 gather_fusion.23
  250.4 2.8 gather_fusion.29
  276.9 3.5 gather_fusion.35
  285.0 3.6 gather_fusion.34
  295.4 3.1 fusion.14
  304.3 7.3 %all-to-all-start.8 = ((f32[16,1,192]{2,1,0:T(1,128)}), f32[16,1,192]{2,1,0:T(1,128)S(1)}, u32[]{:S(2)}, u32[]{:S(2)}) async-start(f32[16,1,192]{2,1,0:T(1,128)} %reshape.796), calls=%async_computation.8 | async-start | bytes 32768 | tf_op jit(solution)/shard_map/all_to_all | solution.py:248
  313.6 4.3 all-to-all-done.8
  317.9 5.8 %all-to-all-start.10 = ((bf16[16,2,48,2,128]{4,3,2,1,0:T(2,128)(2,1)}), bf16[16,2,48,2,128]{4,3,2,1,0:T(2,128)(2,1)}, u32[]{:S(2)}, u32[]{:S(2)}) async-start(bf16[16,2,48,2,128]{4,3,2,1,0:T(2,128)(2,1)} %pad_maximum_fusion.6), calls=%async_computation.10 | async-start | bytes 1572864 | tf_op jit(solution)/shard_map/all_to_all | solution.py:273
  337.3 2.8 select_convert_fusion.1
  345.6 2.9 gather_fusion.27
  349.6 2.9 gather_fusion.31
  354.4 7.3 %all-to-all-start.9 = ((bf16[16,2,48,2,128]{4,3,2,1,0:T(2,128)(2,1)}), bf16[16,2,48,2,128]{4,3,2,1,0:T(2,128)(2,1)S(1)}, u32[]{:S(2)}, u32[]{:S(2)}) async-start(bf16[16,2,48,2,128]{4,3,2,1,0:T(2,128)(2,1)} %pad_maximum_fusion.5), calls=%async_computation.9 | async-start | bytes 1572864 | tf_op jit(solution)/shard_map/all_to_all | solution.py:270
  368.1 3.4 fusion.1
  377.8 3.4 fusion
  383.7 6.3 %copy.572 = bf16[16,2,256,256]{3,2,0,1:T(8,128)(2,1)} copy(bf16[16,2,256,256]{2,3,1,0:T(8,128)(2,1)} %all-to-all-done.1) | data formatting | bytes 8388608 | tf_op jit(solution)/shard_map/all_to_all | solution.py:135
  393.9 3.3 add_convert_fusion
  398.9 70.0 %reduce-scatter.5.cloned.1.call-done = bf16[256,2,256]{0,2,1:T(8,128)(2,1)} async-done(((bf16[4096,2,256]{0,2,1:T(8,128)(2,1)}), bf16[256,2,256]{0,2,1:T(8,128)(2,1)}) %reduce-scatter.5.cloned.1.call-update) | async-done | bytes 262160 | tf_op jit(solution)/shard_map/reduce_scatter | solution.py:300
  471.6 63.1 %reduce-scatter.3.cloned.1.call-done = bf16[512,256]{1,0:T(8,128)(2,1)} async-done(((bf16[512,4096]{1,0:T(8,128)(2,1)}), bf16[512,256]{1,0:T(8,128)(2,1)}) %reduce-scatter.3.cloned.1.call-update) | async-done | bytes 262160 | tf_op jit(solution)/shard_map/reduce_scatter | solution.py:290
  (398 shorter events, 169.1 us)
Async XLA Ops:
  7.2 94.5 %all-gather.2.cloned.1.call-start = ((), (), s32[]{:S(2)}) async-start(), calls=%async_computation.13 | async-start | bytes 4456448 | tf_op jit(solution)/shard_map/all_gather | solution.py:129
  18.9 14.7 %all-to-all-start = ((s32[16,2,48]{2,1,0:T(2,128)}), s32[16,2,48]{2,1,0:T(2,128)S(1)}, u32[]{:S(2)}, u32[]{:S(2)}) async-start(s32[16,2,48]{2,1,0:T(2,128)} %pad_add_fusion), calls=%async_computation | async-start | bytes 32768 | tf_op jit(solution)/shard_map/all_to_all | solution.py:166
  33.2 2.8 copy-start.6
  36.0 60.9 %all-to-all-start.1 = ((bf16[16,2,256,256]{2,3,1,0:T(8,128)(2,1)}), bf16[16,2,256,256]{2,3,1,0:T(8,128)(2,1)}, u32[]{:S(2)}, u32[]{:S(2)}) async-start(bf16[16,2,256,256]{2,3,1,0:T(8,128)(2,1)} %stack.92), calls=%async_computation.1 | async-start | bytes 8388608 | tf_op jit(solution)/shard_map/all_to_all | solution.py:135
  46.8 89.0 %copy-start.31 = (s32[1024]{0:T(1024)}, s32[1024]{0:T(1024)S(1)}, u32[]{:S(2)}) copy-start(s32[1024]{0:T(1024)S(1)} %pad_clamp_fusion.6) | copy-start | bytes 12292
  114.9 25.0 %all-to-all-start.2 = ((bf16[16,2,48,2,128]{4,2,3,1,0:T(8,128)(2,1)}), bf16[16,2,48,2,128]{4,2,3,1,0:T(8,128)(2,1)S(1)}, u32[]{:S(2)}, u32[]{:S(2)}) async-start(bf16[16,2,48,2,128]{4,2,3,1,0:T(8,128)(2,1)} %copy.577), calls=%async_computation.2 | async-start | bytes 1572864 | tf_op jit(solution)/shard_map/all_to_all | solution.py:208
  131.9 65.1 %copy-start.33 = (s32[1024]{0:T(1024)}, s32[1024]{0:T(1024)S(1)}, u32[]{:S(2)}) copy-start(s32[1024]{0:T(1024)S(1)} %pad_clamp_fusion.2) | copy-start | bytes 12292
  139.9 18.5 %all-to-all-start.4 = ((bf16[16,2,48,2,128]{4,2,3,1,0:T(8,128)(2,1)}), bf16[16,2,48,2,128]{4,2,3,1,0:T(8,128)(2,1)S(1)}, u32[]{:S(2)}, u32[]{:S(2)}) async-start(bf16[16,2,48,2,128]{4,2,3,1,0:T(8,128)(2,1)} %copy.610), calls=%async_computation.4 | async-start | bytes 1572864 | tf_op jit(solution)/shard_map/all_to_all | solution.py:209
  157.7 12.8 %copy-start.27 = (bf16[640,2,128]{2,0,1:T(8,128)(2,1)}, bf16[640,2,128]{2,0,1:T(8,128)(2,1)S(1)}, u32[]{:S(2)}) copy-start(bf16[640,2,128]{2,0,1:T(8,128)(2,1)S(1)} %slice.416) | copy-start | bytes 983044
  158.4 12.1 %copy-start.37 = (bf16[1,128,2,128]{3,1,2,0:T(8,128)(2,1)}, bf16[1,128,2,128]{3,1,2,0:T(8,128)(2,1)S(1)}, u32[]{:S(2)}) copy-start(bf16[1,128,2,128]{3,1,2,0:T(8,128)(2,1)S(1)} %slice_bitcast_fusion.4) | copy-start | bytes 196612
  165.7 4.5 copy-start.65
  167.2 3.4 copy-start.56
  167.2 3.4 copy-start.68
  171.3 2.9 copy-start.62
  172.6 2.4 copy-start.64
  176.9 17.7 %copy-start.8 = (f32[6,2,128,256]{3,2,1,0:T(8,128)}, f32[6,2,128,256]{3,2,1,0:T(8,128)S(1)}, u32[]{:S(2)}) copy-start(f32[6,2,128,256]{3,2,1,0:T(8,128)S(1)} %get-tuple-element.91) | copy-start | bytes 4718596
  184.7 19.5 %all-to-all-start.3 = ((f32[16,1,192]{2,1,0:T(1,128)}), f32[16,1,192]{2,1,0:T(1,128)}, u32[]{:S(2)}, u32[]{:S(2)}) async-start(f32[16,1,192]{2,1,0:T(1,128)} %reshape.794), calls=%async_computation.3 | async-start | bytes 32768 | tf_op jit(solution)/shard_map/all_to_all | solution.py:225
  196.3 3.9 copy-start.17
  200.9 12.8 %copy-start.50 = (s32[1024]{0:T(1024)S(1)}, s32[1024]{0:T(1024)}, u32[]{:S(2)}) copy-start(s32[1024]{0:T(1024)} %pad_clamp_fusion) | copy-start | bytes 12292
  204.2 21.0 %all-to-all-start.7 = ((bf16[16,2,48,2,128]{4,3,2,1,0:T(2,128)(2,1)}), bf16[16,2,48,2,128]{4,3,2,1,0:T(2,128)(2,1)S(1)}, u32[]{:S(2)}, u32[]{:S(2)}) async-start(bf16[16,2,48,2,128]{4,3,2,1,0:T(2,128)(2,1)} %pad_maximum_fusion.4), calls=%async_computation.7 | async-start | bytes 1572864 | tf_op jit(solution)/shard_map/all_to_all | solution.py:254
  218.8 2.7 copy-start
  225.2 10.7 %copy-start.2 = (bf16[16,2,48,2,128]{4,3,2,1,0:T(2,128)(2,1)}, bf16[16,2,48,2,128]{4,3,2,1,0:T(2,128)(2,1)S(1)}, u32[]{:S(2)}) copy-start(bf16[16,2,48,2,128]{4,3,2,1,0:T(2,128)(2,1)S(1)} %all-to-all-done.7) | copy-start | bytes 2359300
  225.2 13.5 %all-to-all-start.6 = ((f32[16,1,192]{2,1,0:T(1,128)}), f32[16,1,192]{2,1,0:T(1,128)S(1)}, u32[]{:S(2)}, u32[]{:S(2)}) async-start(f32[16,1,192]{2,1,0:T(1,128)} %reshape.798), calls=%async_computation.6 | async-start | bytes 32768 | tf_op jit(solution)/shard_map/all_to_all | solution.py:247
  239.3 49.4 %all-to-all-start.5 = ((f32[16,2,48,2,128]{4,3,2,1,0:T(2,128)}), f32[16,2,48,2,128]{4,3,2,1,0:T(2,128)S(1)}, u32[]{:S(2)}, u32[]{:S(2)}) async-start(f32[16,2,48,2,128]{4,3,2,1,0:T(2,128)} %pad_maximum_fusion.1), calls=%async_computation.5 | async-start | bytes 3145728 | tf_op jit(solution)/shard_map/all_to_all | solution.py:222
  260.4 2.5 copy-start.67
  269.3 2.6 copy-start.66
  269.3 4.2 copy-start.12
  273.7 3.3 copy-start.34
  288.7 4.0 copy-start.51
  290.0 5.4 copy-start.1
  292.7 5.8 %copy-start.7 = (bf16[512,2,128]{2,1,0:T(2,128)(2,1)S(1)}, bf16[512,2,128]{2,1,0:T(2,128)(2,1)}, u32[]{:S(2)}) copy-start(bf16[512,2,128]{2,1,0:T(2,128)(2,1)} %copy-done.6) | copy-start | bytes 786436
  301.6 10.0 %copy-start.14 = (bf16[768,2,128]{2,1,0:T(2,128)(2,1)S(1)}, bf16[768,2,128]{2,1,0:T(2,128)(2,1)}, u32[]{:S(2)}) copy-start(bf16[768,2,128]{2,1,0:T(2,128)(2,1)} %gather_fusion.35) | copy-start | bytes 1179652
  301.6 10.0 %copy-start.15 = (bf16[768,2,128]{2,1,0:T(2,128)(2,1)S(1)}, bf16[768,2,128]{2,1,0:T(2,128)(2,1)}, u32[]{:S(2)}) copy-start(bf16[768,2,128]{2,1,0:T(2,128)(2,1)} %gather_fusion.34) | copy-start | bytes 1179652
  304.3 13.5 %all-to-all-start.8 = ((f32[16,1,192]{2,1,0:T(1,128)}), f32[16,1,192]{2,1,0:T(1,128)S(1)}, u32[]{:S(2)}, u32[]{:S(2)}) async-start(f32[16,1,192]{2,1,0:T(1,128)} %reshape.796), calls=%async_computation.8 | async-start | bytes 32768 | tf_op jit(solution)/shard_map/all_to_all | solution.py:248
  317.9 36.5 %all-to-all-start.10 = ((bf16[16,2,48,2,128]{4,3,2,1,0:T(2,128)(2,1)}), bf16[16,2,48,2,128]{4,3,2,1,0:T(2,128)(2,1)}, u32[]{:S(2)}, u32[]{:S(2)}) async-start(bf16[16,2,48,2,128]{4,3,2,1,0:T(2,128)(2,1)} %pad_maximum_fusion.6), calls=%async_computation.10 | async-start | bytes 1572864 | tf_op jit(solution)/shard_map/all_to_all | solution.py:273
  325.3 3.4 copy-start.10
  333.8 3.4 copy-start.59
  337.3 2.8 copy-start.26
  337.3 2.8 copy-start.29
  337.3 2.8 copy-start.39
  345.0 3.6 copy-start.3
  345.0 3.6 copy-start.47
  345.1 3.6 copy-start.43
  354.4 9.0 %copy-start.55 = (s32[1024]{0:T(1024)S(1)}, s32[1024]{0:T(1024)}, u32[]{:S(2)}) copy-start(s32[1024]{0:T(1024)} %pad_clamp_fusion.1) | copy-start | bytes 12292
  354.4 11.4 %copy-start.52 = (s32[1024]{0:T(1024)S(1)}, s32[1024]{0:T(1024)}, u32[]{:S(2)}) copy-start(s32[1024]{0:T(1024)} %pad_clamp_fusion) | copy-start | bytes 12292
  354.4 17.4 %all-to-all-start.9 = ((bf16[16,2,48,2,128]{4,3,2,1,0:T(2,128)(2,1)}), bf16[16,2,48,2,128]{4,3,2,1,0:T(2,128)(2,1)S(1)}, u32[]{:S(2)}, u32[]{:S(2)}) async-start(bf16[16,2,48,2,128]{4,3,2,1,0:T(2,128)(2,1)} %pad_maximum_fusion.5), calls=%async_computation.9 | async-start | bytes 1572864 | tf_op jit(solution)/shard_map/all_to_all | solution.py:270
  361.7 107.2 %reduce-scatter.5.cloned.1.call-start = ((), (), s32[]{:S(2)}) async-start(), calls=%async_computation.15 | async-start | bytes 4456448 | tf_op jit(solution)/shard_map/reduce_scatter | solution.py:300
  383.7 151.0 %reduce-scatter.3.cloned.1.call-start = ((), (), s32[]{:S(2)}) async-start(), calls=%async_computation.14 | async-start | bytes 4456448 | tf_op jit(solution)/shard_map/reduce_scatter | solution.py:290
  (35 other events, 47.6 us)
Sparse Core Ops, SparseCore 0:
  9.8 52.7 all-gather.1
  383.8 85.0 reduce-scatter.4
  472.2 62.4 reduce-scatter.2
